TPU v7x, 32 devices: a whole 2x2x4 slice. The times are simulated.
32 devices in a mesh: dp: 8 (over z, y), tensor: 4 (over x, core).
Axes of the slice: x: 2, y: 2, z: 4, core: 2. Of those that a mesh axis runs over, the one named last changes fastest.
Arguments:
- tokens: bfloat16 [2048, 1024], P('dp'), may hold values from -6 to 6
- norm_first: float32 [1024], replicated, may hold values from 0.25 to 1.75
- w_in: bfloat16 [1024, 3, 1024], P(None, None, 'tensor'), may hold values from -0.1875 to 0.1875
- conv_taps: float32 [3, 1024], P(None, 'tensor'), may hold values from -1 to 1
- w_out: bfloat16 [1024, 1024], P('tensor'), may hold values from -0.1875 to 0.1875
- norm_second: float32 [1024], replicated, may hold values from 0.25 to 1.75
- w_gate_up: bfloat16 [1024, 2, 4608], P(None, None, 'tensor'), may hold values from -0.1875 to 0.1875
- w_down: bfloat16 [4608, 1024], P('tensor'), may hold values from -0.09375 to 0.09375
- cotangent: bfloat16 [2048, 1024], P('dp'), may hold values from -6 to 6
Outputs:
- block_out: bfloat16 [2048, 1024], P('dp')
- grad_tokens: float32 [2048, 1024], P('dp')
- grad_norm_first: float32 [1024], replicated
- grad_w_in: float32 [1024, 3, 1024], P('dp', None, 'tensor')
- grad_taps: float32 [3, 1024], P(None, 'tensor')
- grad_w_out: float32 [1024, 1024], P('tensor', 'dp')
- grad_norm_second: float32 [1024], replicated
- grad_w_gate_up: float32 [1024, 2, 4608], P('dp', None, 'tensor')
- grad_w_down: float32 [4608, 1024], P('tensor', 'dp')
All inputs are finite; a program needn't handle non-finite values.
Results may differ from a plain program's by a relative error of at most 0.011.
Values sent between devices are 32-bit elements; how exact they have to be, the bound alone decides.
No kernel may reach another device: no remote copies, remote signals or barrier semaphores. Data moves between devices by JAX's collectives and lax.ppermute only.
A program may use at most 128 MiB of HBM per device.

v0:
```python
import jax
import jax.numpy as jnp
from jax import lax
from jax.sharding import PartitionSpec as P

eps = 1e-05


def shift_down(values, count):
    pad = jnp.zeros((count, values.shape[1]), values.dtype)
    return jnp.concatenate([pad, values[: values.shape[0] - count]], axis=0)


def shift_up(values, count):
    pad = jnp.zeros((count, values.shape[1]), values.dtype)
    return jnp.concatenate([values[count:], pad], axis=0)


def cross(left, right):
    return lax.dot_general(
        left, right, (((0,), (0,)), ((), ())), preferred_element_type=jnp.float32
    )


def by_transpose(left, right):
    return lax.dot_general(
        left, right, (((1,), (1,)), ((), ())), preferred_element_type=jnp.float32
    )


def body(tokens, norm_first, w_in, conv_taps, w_out, norm_second, w_gate_up, w_down, cotangent):
    rows, width = tokens.shape
    chans = w_in.shape[2]
    hid = w_down.shape[0]
    w_in_flat = w_in.reshape(width, 3 * chans)
    w_gu_flat = w_gate_up.reshape(width, 2 * hid)
    xf = tokens.astype(jnp.float32)
    s1 = lax.rsqrt(jnp.mean(xf * xf, axis=-1, keepdims=True) + eps)
    normed1 = (xf * s1 * norm_first).astype(jnp.bfloat16)
    proj = jnp.dot(normed1, w_in_flat, preferred_element_type=jnp.float32).reshape(rows, 3, chans)
    gate_b, gate_c, value = (proj[:, 0], proj[:, 1], proj[:, 2])
    mixed_in = gate_b * value
    conv = (
        conv_taps[0] * shift_down(mixed_in, 2)
        + conv_taps[1] * shift_down(mixed_in, 1)
        + conv_taps[2] * mixed_in
    )
    gated = (gate_c * conv).astype(jnp.bfloat16)
    mix = lax.psum(jnp.dot(gated, w_out, preferred_element_type=jnp.float32), "tensor")
    resid = xf + mix
    s2 = lax.rsqrt(jnp.mean(resid * resid, axis=-1, keepdims=True) + eps)
    normed2 = (resid * s2 * norm_second).astype(jnp.bfloat16)
    gate_up = jnp.dot(normed2, w_gu_flat, preferred_element_type=jnp.float32).reshape(rows, 2, hid)
    act, up = (gate_up[:, 0], gate_up[:, 1])
    sig = jax.nn.sigmoid(act)
    hidden = (act * sig * up).astype(jnp.bfloat16)
    ffn = lax.psum(jnp.dot(hidden, w_down, preferred_element_type=jnp.float32), "tensor")
    block_out = (resid + ffn).astype(jnp.bfloat16)
    cotf = cotangent.astype(jnp.float32)
    grad_down = cross(hidden, cotangent)
    d_hidden = by_transpose(cotangent, w_down)
    d_act = d_hidden * up * sig * (1.0 + act * (1.0 - sig))
    d_up = d_hidden * act * sig
    d_gu = jnp.stack([d_act, d_up], axis=1).astype(jnp.bfloat16).reshape(rows, 2 * hid)
    grad_gu = cross(normed2, d_gu).reshape(width, 2, hid)
    d_normed2 = lax.psum(by_transpose(d_gu, w_gu_flat), "tensor")
    gn2 = jnp.sum(d_normed2 * resid * s2, axis=0)
    weighted2 = d_normed2 * norm_second
    d_resid = (
        cotf + s2 * weighted2 - resid * s2**3 * jnp.mean(weighted2 * resid, axis=-1, keepdims=True)
    )
    d_resid_b = d_resid.astype(jnp.bfloat16)
    grad_out = cross(gated, d_resid_b)
    d_gated = by_transpose(d_resid_b, w_out)
    d_c = d_gated * conv
    d_conv = d_gated * gate_c
    gtaps = jnp.stack(
        [
            jnp.sum(d_conv * shift_down(mixed_in, 2), axis=0),
            jnp.sum(d_conv * shift_down(mixed_in, 1), axis=0),
            jnp.sum(d_conv * mixed_in, axis=0),
        ],
        axis=0,
    )
    d_mixed = (
        conv_taps[2] * d_conv
        + conv_taps[1] * shift_up(d_conv, 1)
        + conv_taps[0] * shift_up(d_conv, 2)
    )
    d_proj = (
        jnp.stack([d_mixed * value, d_c, d_mixed * gate_b], axis=1)
        .astype(jnp.bfloat16)
        .reshape(rows, 3 * chans)
    )
    grad_in = cross(normed1, d_proj).reshape(width, 3, chans)
    d_normed1 = lax.psum(by_transpose(d_proj, w_in_flat), "tensor")
    gn1 = jnp.sum(d_normed1 * xf * s1, axis=0)
    weighted1 = d_normed1 * norm_first
    grad_tokens = (
        d_resid + s1 * weighted1 - xf * s1**3 * jnp.mean(weighted1 * xf, axis=-1, keepdims=True)
    )
    shared_in, shared_out, shared_gu, shared_down = (
        lax.psum_scatter(grad_in, "dp", scatter_dimension=0, tiled=True),
        lax.psum_scatter(grad_out, "dp", scatter_dimension=1, tiled=True),
        lax.psum_scatter(grad_gu, "dp", scatter_dimension=0, tiled=True),
        lax.psum_scatter(grad_down, "dp", scatter_dimension=1, tiled=True),
    )
    sum_taps, sum_n1, sum_n2 = lax.psum((gtaps, gn1, gn2), "dp")
    return (
        block_out,
        grad_tokens,
        sum_n1,
        shared_in,
        sum_taps,
        shared_out,
        sum_n2,
        shared_gu,
        shared_down,
    )


def solution(mesh):
    return jax.shard_map(
        body,
        mesh=mesh,
        in_specs=(
            P("dp", None),
            P(),
            P(None, None, "tensor"),
            P(None, "tensor"),
            P("tensor", None),
            P(),
            P(None, None, "tensor"),
            P("tensor", None),
            P("dp", None),
        ),
        out_specs=(
            P("dp", None),
            P("dp", None),
            P(),
            P("dp", None, "tensor"),
            P(None, "tensor"),
            P("tensor", "dp"),
            P(),
            P("dp", None, "tensor"),
            P("tensor", "dp"),
        ),
        check_vma=False,
    )
```

profile of v0, /device:TPU:0, one launch (start us, length us, event | category | flops | bytes accessed | tf_op | source)
XLA Modules:
  0.0 582.6 jit_solution(139281299403452561)
XLA Ops:
  7.2 1.4 fusion.9
  10.0 2.7 copy.24
  12.7 2.1 fusion.2
  16.3 1.3 fusion.34
  17.6 5.4 copy.37
  23.0 6.7 %copy.25 = bf16[2304,1024]{1,0:T(8,128)(2,1)} copy(bf16[2304,1024]{0,1:T(8,128)(2,1)} %bitcast.107) | data formatting | bytes 9437184 | tf_op jit(solution)/shard_map/dot_general | solution.py:53
  29.6 27.1 %all-reduce.10.cloned.1.call-done = f32[256,1024]{1,0:T(8,128)} async-done(((f32[256,1024]{1,0:T(8,128)}), f32[256,1024]{1,0:T(8,128)}) %all-reduce.10.cloned.1.call-update) | async-done | bytes 1048592 | tf_op jit(solution)/shard_map/psum | solution.py:49
  56.8 1.6 multiply_reduce_fusion.2
  58.9 3.9 fusion.30
  62.9 1.2 multiply_bitcast_fusion.1
  65.3 2.4 fusion.4
  67.8 2.0 multiply_convert_fusion
  70.6 1.9 fusion.35
  72.5 32.2 %all-reduce.12.cloned.1.call-done = f32[256,1024]{1,0:T(8,128)} async-done(((f32[256,1024]{1,0:T(8,128)}), f32[256,1024]{1,0:T(8,128)}) %all-reduce.12.cloned.1.call-update) | async-done | bytes 1048592 | tf_op jit(solution)/shard_map/psum | solution.py:66
  104.7 1.6 multiply_reduce_fusion
  107.7 1.1 multiply_reduce_fusion.5
  110.7 1.6 convolution_bitcast_fusion
  112.6 2.4 maximum_convert_fusion
  115.0 2.4 copy.29
  117.4 6.8 %fusion.7 = f32[1024,2,1152]{2,0,1:T(8,128)} fusion(bf16[256,2,1152]{0,2,1:T(8,128)(2,1)} %copy.29, f32[256,1024]{1,0:T(8,128)S(1)} %get-tuple-element.43, f32[1024]{0:T(1024)S(1)} %copy-done.21, f32[256]{0:T(256)S(1)} %get-tuple-element.54), kind=kOutput, calls=%fused_computation.15 | convolution fusion | flops 1208745984 | bytes 11670528 | tf_op jit(solution)/shard_map/dot_general | solution.py:20
  124.3 2.5 fusion.23
  126.9 3.5 fusion.19
  130.5 4.2 fusion.36
  135.5 28.9 %all-reduce.14.cloned.1.call-done = (f32[256,1024]{1,0:T(8,128)}, f32[256,1024]{1,0:T(8,128)}) async-done(((f32[256,1024]{1,0:T(8,128)}, f32[256,1024]{1,0:T(8,128)}), (f32[256,1024]{1,0:T(8,128)}, f32[256,1024]{1,0:T(8,128)})) %all-reduce.14.cloned.1.call-update) | async-done | bytes 2097168 | tf_op jit(solution)/shard_map/psum | solution.py:57
  164.4 1.7 fusion.16
  166.1 39.2 %all-reduce.4 = (f32[1024]{0:T(1024)}, f32[3,256]{1,0:T(4,128)}, f32[1024]{0:T(1024)}) all-reduce(f32[1024]{0:T(1024)S(1)} %get-tuple-element.29, f32[3,256]{1,0:T(4,128)S(1)} %pad_maximum_fusion, f32[1024]{0:T(1024)S(1)} %get-tuple-element.27), channel_id=1, replica_groups=mesh['dp'=8,'tensor'=4] {'dp'}, use_global_device_ids=true, to_apply=%region_9.0 | all-reduce | flops 2816 | bytes 22528 | tf_op jit(solution)/shard_map/psum | solution.py:108
  205.3 3.5 fusion.13
  208.7 121.8 %reduce-scatter.9.cloned.1.call-done = f32[128,2,1152]{2,0,1:T(8,128)} async-done(((f32[1024,2,1152]{2,0,1:T(8,128)}), f32[128,2,1152]{2,0,1:T(8,128)}) %reduce-scatter.9.cloned.1.call-update) | async-done | bytes 1179664 | tf_op jit(solution)/shard_map/reduce_scatter | solution.py:105
  330.6 3.2 copy.31
  333.8 64.5 %reduce-scatter.7.cloned.1.call-done = f32[256,128]{1,0:T(8,128)} async-done(((f32[256,1024]{1,0:T(8,128)}), f32[256,128]{1,0:T(8,128)}) %reduce-scatter.7.cloned.1.call-update) | async-done | bytes 131088 | tf_op jit(solution)/shard_map/reduce_scatter | solution.py:104
  398.3 77.9 %reduce-scatter.5.cloned.1.call-done = f32[128,3,256]{2,0,1:T(8,128)} async-done(((f32[1024,3,256]{2,0,1:T(8,128)}), f32[128,3,256]{2,0,1:T(8,128)}) %reduce-scatter.5.cloned.1.call-update) | async-done | bytes 393232 | tf_op jit(solution)/shard_map/reduce_scatter | solution.py:103
  476.2 99.5 %reduce-scatter.11.cloned.1.call-done = f32[1152,128]{1,0:T(8,128)} async-done(((f32[1152,1024]{1,0:T(8,128)}), f32[1152,128]{1,0:T(8,128)}) %reduce-scatter.11.cloned.1.call-update) | async-done | bytes 589840 | tf_op jit(solution)/shard_map/reduce_scatter | solution.py:106
  (105 shorter events, 10.0 us)
Async XLA Ops:
  7.2 55.7 %copy-start = (bf16[1152,1024]{1,0:T(8,128)(2,1)S(1)}, bf16[1152,1024]{1,0:T(8,128)(2,1)}, u32[]{:S(2)}) copy-start(bf16[1152,1024]{1,0:T(8,128)(2,1)} %param.16) | copy-start | bytes 7077892
  7.2 49.6 %all-reduce.10.cloned.1.call-start = ((), (), s32[]{:S(2)}) async-start(), calls=%async_computation.4 | async-start | bytes 2097152 | tf_op jit(solution)/shard_map/psum | solution.py:49
  9.2 3.5 copy-start.23
  10.0 4.9 copy-start.25
  10.0 4.9 copy-start.27
  10.0 4.9 copy-start.29
  10.0 2.7 copy-start.2
  10.0 2.7 copy-start.22
  14.8 1.4 copy-start.11
  14.9 2.7 copy-start.3
  17.6 87.1 %all-reduce.12.cloned.1.call-start = ((), (), s32[]{:S(2)}) async-start(), calls=%async_computation.5 | async-start | bytes 2097152 | tf_op jit(solution)/shard_map/psum | solution.py:66
  29.6 29.3 %copy-start.21 = (f32[1024]{0:T(1024)S(1)}, f32[1024]{0:T(1024)}, u32[]{:S(2)}) copy-start(f32[1024]{0:T(1024)} %param.14) | copy-start | bytes 12292
  58.9 4.0 copy-start.13
  58.9 6.4 %slice-start = ((s8[4718592]{0:T(1024)(128)(4,1)}), s8[4194304]{0:T(1024)(128)(4,1)S(1)}, s32[]{:S(2)}) async-start(s8[4718592]{0:T(1024)(128)(4,1)} %bitcast.114), calls=%async_computation.11 | async-start | bytes 8388608
  62.9 1.4 copy-start.5
  62.9 2.4 slice-start.1
  67.8 96.7 %all-reduce.14.cloned.1.call-start = ((), (), s32[]{:S(2)}) async-start(), calls=%async_computation.10 | async-start | bytes 4194304 | tf_op jit(solution)/shard_map/psum | solution.py:57
  104.7 1.6 copy-start.10
  104.7 1.7 copy-start.14
  104.7 1.7 copy-start.34
  106.3 1.2 copy-start.9
  106.3 1.4 copy-start.12
  107.7 1.4 copy-start.26
  107.7 1.4 copy-start.28
  107.7 1.4 copy-start.30
  109.1 1.6 copy-start.7
  112.4 218.2 %reduce-scatter.9.cloned.1.call-start = ((), (), s32[]{:S(2)}) async-start(), calls=%async_computation.8 | async-start | bytes 10616832 | tf_op jit(solution)/shard_map/reduce_scatter | solution.py:105
  124.2 2.7 copy-start.24
  124.2 274.1 %reduce-scatter.7.cloned.1.call-start = ((), (), s32[]{:S(2)}) async-start(), calls=%async_computation.7 | async-start | bytes 1179648 | tf_op jit(solution)/shard_map/reduce_scatter | solution.py:104
  126.8 349.4 %reduce-scatter.5.cloned.1.call-start = ((), (), s32[]{:S(2)}) async-start(), calls=%async_computation.6 | async-start | bytes 3538944 | tf_op jit(solution)/shard_map/reduce_scatter | solution.py:103
  130.5 445.3 %reduce-scatter.11.cloned.1.call-start = ((), (), s32[]{:S(2)}) async-start(), calls=%async_computation.9 | async-start | bytes 5308416 | tf_op jit(solution)/shard_map/reduce_scatter | solution.py:106
  134.8 70.5 %copy-start.35 = (f32[256]{0:T(256)S(1)}, f32[256]{0:T(256)}, u32[]{:S(2)}) copy-start(f32[256]{0:T(256)} %get-tuple-element.51) | copy-start | bytes 3076
  (13 other events, 11.1 us)
Sparse Core Ops, SparseCore 0:
  17.7 39.0 all-reduce.9
  67.9 36.7 all-reduce.11
  112.5 51.8 all-reduce.13
  167.9 162.6 reduce-scatter.8
  334.4 63.8 reduce-scatter.6
  402.3 73.8 reduce-scatter.4
  480.4 95.2 reduce-scatter.10
where the time goes:
time: 583 us
  waiting for transfers between devices  452 us (78%)
  blocking collectives  39.2 us (7%)
  matrix products  32.6 us (6%)
  local copies, waits for them, and re-layouts  26.8 us (5%)
  other arithmetic  16.9 us (3%)
  between operations  14.5 us (2%)
    reduce_scatter x1, waiting for transfers between devices, body(): lax.psum_scatter(grad_gu, 'dp', scatter_dimension=0, tiled=True)  122 us
    reduce_scatter x1, waiting for transfers between devices, body(): lax.psum_scatter(grad_down, 'dp', scatter_dimension=1, tiled=True)  99.5 us
    reduce_scatter x1, waiting for transfers between devices, body(): lax.psum_scatter(grad_in, 'dp', scatter_dimension=0, tiled=True)  77.9 us
    reduce_scatter x1, waiting for transfers between devices, body(): lax.psum_scatter(grad_out, 'dp', scatter_dimension=1, tiled=True)  64.5 us
    psum x1, blocking collectives, body(): sum_taps, sum_n1, sum_n2 = lax.psum((gtaps, gn1, gn2), 'dp')  39.2 us
    psum x1, waiting for transfers between devices, body(): d_normed2 = lax.psum(by_transpose(d_gu, w_gu_flat), 'tensor')  32.2 us
    psum x1, waiting for transfers between devices, body(): lax.psum(jnp.dot(hidden, w_down, preferred_element_type=jnp.float32), 'te...  28.9 us
    psum x1, waiting for transfers between devices, body(): lax.psum(jnp.dot(gated, w_out, preferred_element_type=jnp.float32), 'tens...  27.1 us
  transfers between devices with their start and end apart: 7, of which 7 were waited for; matrix products, arithmetic and copies ran while one was open for 8% of the time, Pallas kernels for 0%

commit v1 on v0

--- a/solution.py
+++ b/solution.py
@@ -63,7 +63,8 @@
     d_up = d_hidden * act * sig
     d_gu = jnp.stack([d_act, d_up], axis=1).astype(jnp.bfloat16).reshape(rows, 2 * hid)
     grad_gu = cross(normed2, d_gu).reshape(width, 2, hid)
-    d_normed2 = lax.psum(by_transpose(d_gu, w_gu_flat), "tensor")
+    my_data = by_transpose(d_gu, w_gu_flat)
+    d_normed2 = lax.all_gather(my_data, "tensor").sum(axis=0)
     gn2 = jnp.sum(d_normed2 * resid * s2, axis=0)
     weighted2 = d_normed2 * norm_second
     d_resid = (

time: 583 us -> 584 us (level)
    psum x1 -> x0, waiting for transfers between devices: 32.2 us -> none  [body(): d_normed2 = lax.psum(by_transpose(d_gu, w_gu_flat), 'tensor')]
    all_gather x0 -> x1, waiting for transfers between devices: none -> 30.4 us  [body(): d_normed2 = lax.all_gather(my_data, 'tensor').sum(axis=0)]
    unnamed x79 -> x87, local copies, waits for them, and re-layouts: 16.7 us -> 18.4 us
  transfers between devices with their start and end apart: 7 -> 7, of which waited for: 7 -> 7; matrix products, arithmetic and copies ran while one was open for 8% -> 7% of each run, Pallas kernels for 0% -> 0%
where the time goes in v1:
time: 584 us; the launch traced here: 583 us
  waiting for transfers between devices  455 us (78%)
  blocking collectives  39.2 us (7%)
  matrix products  28.6 us (5%)
  local copies, waits for them, and re-layouts  27.5 us (5%)
  other arithmetic  17.3 us (3%)
  between operations  14.5 us (2%)
    reduce_scatter x1, waiting for transfers between devices, body(): lax.psum_scatter(grad_gu, 'dp', scatter_dimension=0, tiled=True)  122 us
    reduce_scatter x1, waiting for transfers between devices, body(): lax.psum_scatter(grad_down, 'dp', scatter_dimension=1, tiled=True)  99.2 us
    reduce_scatter x1, waiting for transfers between devices, body(): lax.psum_scatter(grad_in, 'dp', scatter_dimension=0, tiled=True)  78.7 us
    reduce_scatter x1, waiting for transfers between devices, body(): lax.psum_scatter(grad_out, 'dp', scatter_dimension=1, tiled=True)  64.5 us
    psum x1, blocking collectives, body(): sum_taps, sum_n1, sum_n2 = lax.psum((gtaps, gn1, gn2), 'dp')  39.2 us
    psum x1, waiting for transfers between devices, body(): lax.psum(jnp.dot(hidden, w_down, preferred_element_type=jnp.float32), 'te...  33.3 us
    all_gather x1, waiting for transfers between devices, body(): d_normed2 = lax.all_gather(my_data, 'tensor').sum(axis=0)  30.4 us
    psum x1, waiting for transfers between devices, body(): lax.psum(jnp.dot(gated, w_out, preferred_element_type=jnp.float32), 'tens...  27.1 us
  transfers between devices with their start and end apart: 7, of which 7 were waited for; matrix products, arithmetic and copies ran while one was open for 7% of the time, Pallas kernels for 0%

profile of v1, /device:TPU:0, one launch (start us, length us, event | category | flops | bytes accessed | tf_op | source)
XLA Modules:
  0.0 582.8 jit_solution(18272814526753728526)
XLA Ops:
  7.2 1.4 fusion.9
  10.1 2.7 copy.24
  12.7 2.1 fusion.2
  16.3 1.3 fusion.34
  17.7 5.4 copy.37
  23.0 6.7 %copy.25 = bf16[2304,1024]{1,0:T(8,128)(2,1)} copy(bf16[2304,1024]{0,1:T(8,128)(2,1)} %bitcast.108) | data formatting | bytes 9437184 | tf_op jit(solution)/shard_map/dot_general | solution.py:53
  29.7 27.1 %all-reduce.9.cloned.1.call-done = f32[256,1024]{1,0:T(8,128)} async-done(((f32[256,1024]{1,0:T(8,128)}), f32[256,1024]{1,0:T(8,128)}) %all-reduce.9.cloned.1.call-update) | async-done | bytes 1048592 | tf_op jit(solution)/shard_map/psum | solution.py:49
  56.8 1.6 multiply_reduce_fusion.2
  58.9 3.9 fusion.30
  62.9 1.2 multiply_bitcast_fusion.1
  65.4 2.4 fusion.4
  67.9 2.0 multiply_convert_fusion
  70.6 1.9 fusion.35
  72.5 30.4 %all-gather.3.cloned.1.call-done = f32[1024,1024]{1,0:T(8,128)} async-done(((f32[256,1024]{1,0:T(8,128)}), f32[1024,1024]{1,0:T(8,128)}) %all-gather.3.cloned.1.call-update) | async-done | bytes 4194320 | tf_op jit(solution)/shard_map/all_gather | solution.py:67
  102.9 2.7 reduce_sum.92
  108.0 1.1 multiply_reduce_fusion.5
  111.0 1.6 convolution_bitcast_fusion
  112.9 1.4 maximum_convert_fusion
  114.3 1.4 copy.29
  115.7 6.5 %fusion.7 = f32[1024,2,1152]{2,0,1:T(8,128)} fusion(bf16[256,2,1152]{0,2,1:T(8,128)(2,1)} %copy.29, f32[256,1024]{1,0:T(8,128)S(1)} %get-tuple-element.43, f32[1024]{0:T(1024)S(1)} %copy-done.25, f32[256]{0:T(256)S(1)} %get-tuple-element.54), kind=kOutput, calls=%fused_computation.15 | convolution fusion | flops 1208745984 | bytes 11670528 | tf_op jit(solution)/shard_map/dot_general | solution.py:20
  122.3 1.3 fusion.23
  123.7 3.0 fusion.36
  127.8 2.3 fusion.19
  130.9 33.3 %all-reduce.11.cloned.1.call-done = (f32[256,1024]{1,0:T(8,128)}, f32[256,1024]{1,0:T(8,128)}) async-done(((f32[256,1024]{1,0:T(8,128)}, f32[256,1024]{1,0:T(8,128)}), (f32[256,1024]{1,0:T(8,128)}, f32[256,1024]{1,0:T(8,128)})) %all-reduce.11.cloned.1.call-update) | async-done | bytes 2097168 | tf_op jit(solution)/shard_map/psum | solution.py:57
  164.2 1.5 fusion.16
  165.7 39.2 %all-reduce.4 = (f32[1024]{0:T(1024)}, f32[3,256]{1,0:T(4,128)}, f32[1024]{0:T(1024)}) all-reduce(f32[1024]{0:T(1024)S(1)} %get-tuple-element.29, f32[3,256]{1,0:T(4,128)S(1)} %pad_maximum_fusion, f32[1024]{0:T(1024)S(1)} %get-tuple-element.27), channel_id=1, replica_groups=mesh['dp'=8,'tensor'=4] {'dp'}, use_global_device_ids=true, to_apply=%region_9.0 | all-reduce | flops 2816 | bytes 22528 | tf_op jit(solution)/shard_map/psum | solution.py:109
  205.0 3.6 fusion.13
  208.6 121.7 %reduce-scatter.9.cloned.1.call-done = f32[128,2,1152]{2,0,1:T(8,128)} async-done(((f32[1024,2,1152]{2,0,1:T(8,128)}), f32[128,2,1152]{2,0,1:T(8,128)}) %reduce-scatter.9.cloned.1.call-update) | async-done | bytes 1179664 | tf_op jit(solution)/shard_map/reduce_scatter | solution.py:106
  330.3 3.2 copy.31
  333.5 64.5 %reduce-scatter.7.cloned.1.call-done = f32[256,128]{1,0:T(8,128)} async-done(((f32[256,1024]{1,0:T(8,128)}), f32[256,128]{1,0:T(8,128)}) %reduce-scatter.7.cloned.1.call-update) | async-done | bytes 131088 | tf_op jit(solution)/shard_map/reduce_scatter | solution.py:105
  398.0 99.2 %reduce-scatter.11.cloned.1.call-done = f32[1152,128]{1,0:T(8,128)} async-done(((f32[1152,1024]{1,0:T(8,128)}), f32[1152,128]{1,0:T(8,128)}) %reduce-scatter.11.cloned.1.call-update) | async-done | bytes 589840 | tf_op jit(solution)/shard_map/reduce_scatter | solution.py:107
  497.2 78.7 %reduce-scatter.5.cloned.1.call-done = f32[128,3,256]{2,0,1:T(8,128)} async-done(((f32[1024,3,256]{2,0,1:T(8,128)}), f32[128,3,256]{2,0,1:T(8,128)}) %reduce-scatter.5.cloned.1.call-update) | async-done | bytes 393232 | tf_op jit(solution)/shard_map/reduce_scatter | solution.py:104
  (114 shorter events, 11.9 us)
Async XLA Ops:
  7.2 55.7 %copy-start = (bf16[1152,1024]{1,0:T(8,128)(2,1)S(1)}, bf16[1152,1024]{1,0:T(8,128)(2,1)}, u32[]{:S(2)}) copy-start(bf16[1152,1024]{1,0:T(8,128)(2,1)} %param.16) | copy-start | bytes 7077892
  7.2 49.6 %all-reduce.9.cloned.1.call-start = ((), (), s32[]{:S(2)}) async-start(), calls=%async_computation.4 | async-start | bytes 2097152 | tf_op jit(solution)/shard_map/psum | solution.py:49
  9.2 3.5 copy-start.27
  10.0 4.9 copy-start.29
  10.0 4.9 copy-start.31
  10.0 4.9 copy-start.33
  10.0 2.7 copy-start.3
  10.0 2.7 copy-start.26
  14.9 1.4 copy-start.13
  14.9 2.7 copy-start.5
  17.6 85.3 %all-gather.3.cloned.1.call-start = ((), (), s32[]{:S(2)}) async-start(), calls=%async_computation.9 | async-start | bytes 5242880 | tf_op jit(solution)/shard_map/all_gather | solution.py:67
  29.7 29.2 %copy-start.25 = (f32[1024]{0:T(1024)S(1)}, f32[1024]{0:T(1024)}, u32[]{:S(2)}) copy-start(f32[1024]{0:T(1024)} %param.14) | copy-start | bytes 12292
  58.9 4.0 copy-start.15
  58.9 6.4 %slice-start = ((s8[4718592]{0:T(1024)(128)(4,1)}), s8[4194304]{0:T(1024)(128)(4,1)S(1)}, s32[]{:S(2)}) async-start(s8[4718592]{0:T(1024)(128)(4,1)} %bitcast.115), calls=%async_computation.11 | async-start | bytes 8388608
  62.9 1.5 copy-start.7
  62.9 2.5 slice-start.1
  67.8 96.4 %all-reduce.11.cloned.1.call-start = ((), (), s32[]{:S(2)}) async-start(), calls=%async_computation.10 | async-start | bytes 4194304 | tf_op jit(solution)/shard_map/psum | solution.py:57
  108.0 14.3 %copy-start.2 = (f32[256,1024]{1,0:T(8,128)}, f32[256,1024]{1,0:T(8,128)S(1)}, u32[]{:S(2)}) copy-start(f32[256,1024]{1,0:T(8,128)S(1)} %multiply_subtract_fusion) | copy-start | bytes 3145732
  108.0 1.4 copy-start.30
  108.0 1.4 copy-start.32
  108.0 1.4 copy-start.34
  109.4 1.5 copy-start.10
  109.7 2.9 copy-start.18
  110.4 2.2 copy-start.20
  112.7 217.7 %reduce-scatter.9.cloned.1.call-start = ((), (), s32[]{:S(2)}) async-start(), calls=%async_computation.7 | async-start | bytes 10616832 | tf_op jit(solution)/shard_map/reduce_scatter | solution.py:106
  122.2 1.5 copy-start.9
  122.2 1.5 copy-start.17
  122.2 275.8 %reduce-scatter.7.cloned.1.call-start = ((), (), s32[]{:S(2)}) async-start(), calls=%async_computation.6 | async-start | bytes 1179648 | tf_op jit(solution)/shard_map/reduce_scatter | solution.py:105
  123.6 373.6 %reduce-scatter.11.cloned.1.call-start = ((), (), s32[]{:S(2)}) async-start(), calls=%async_computation.8 | async-start | bytes 5308416 | tf_op jit(solution)/shard_map/reduce_scatter | solution.py:107
  126.7 449.2 %reduce-scatter.5.cloned.1.call-start = ((), (), s32[]{:S(2)}) async-start(), calls=%async_computation.5 | async-start | bytes 3538944 | tf_op jit(solution)/shard_map/reduce_scatter | solution.py:104
  130.2 74.8 %copy-start.39 = (f32[256]{0:T(256)S(1)}, f32[256]{0:T(256)}, u32[]{:S(2)}) copy-start(f32[256]{0:T(256)} %get-tuple-element.51) | copy-start | bytes 3076
  205.0 370.9 %copy-start.1 = (bf16[1152,1024]{1,0:T(8,128)(2,1)S(1)}, bf16[1152,1024]{1,0:T(8,128)(2,1)}, u32[]{:S(2)}) copy-start(bf16[1152,1024]{1,0:T(8,128)(2,1)} %param.16) | copy-start | bytes 7077892
  (17 other events, 16.7 us)
Sparse Core Ops, SparseCore 0:
  17.7 39.0 all-reduce.8
  67.9 34.9 all-gather.2
  112.8 51.3 all-reduce.10
  167.6 162.6 reduce-scatter.8
  334.1 63.8 reduce-scatter.6
  402.1 95.0 reduce-scatter.10
  501.4 74.4 reduce-scatter.4
